TPU v7x, 32 devices: a whole 2x2x4 slice. The times are simulated.
32 devices in a mesh: grp: 2 (over x), dev: 16 (over z, y, core).
Axes of the slice: x: 2, y: 2, z: 4, core: 2. Of those that a mesh axis runs over, the one named last changes fastest.
Arguments:
- query: bfloat16 [64, 64, 128], P(('grp', 'dev')), may hold values from -6 to 6
- key_cache: bfloat16 [64, 512, 8, 128], P(('grp', 'dev')), may hold values from -6 to 6
- value_cache: bfloat16 [64, 512, 8, 128], P(('grp', 'dev')), may hold values from -6 to 6
- lengths: int32 [64], P(('grp', 'dev')), may hold values from 1 to 512, 16384 in all
- out_weight: bfloat16 [8192, 8192], P('dev', 'grp'), may hold values from -0.0625 to 0.0625
- resid: bfloat16 [64, 8192], P('dev', 'grp'), may hold values from -6 to 6
- norm_gain: bfloat16 [8192], P('grp'), may hold values from 0.5 to 1.5
- gate_weight: bfloat16 [8192, 28672], P('grp', 'dev'), may hold values from -0.0625 to 0.0625
- up_weight: bfloat16 [8192, 28672], P('grp', 'dev'), may hold values from -0.0625 to 0.0625
- down_weight: bfloat16 [28672, 8192], P('dev', 'grp'), may hold values from -0.03125 to 0.03125
Outputs:
- layer_out: bfloat16 [64, 8192], P('dev', 'grp')
Inputs may be any that keep to these rules, and one draw needn't show every extreme that they name: `lengths`: some request has exactly 512 live slots.
All inputs are finite; a program needn't handle non-finite values. No bound on the sum of `lengths` on one device may be relied on, other than what follows from the above.
Results may differ from a plain program's by a relative error of at most 0.015.
Values may be sent and summed in bfloat16 or wider, within the bound.
A program may use at most 128 MiB of HBM per device.

v0:
```python
import jax
import jax.numpy as jnp
from jax import lax
from jax.sharding import PartitionSpec as P


def attend(query, key_cache, value_cache, lengths):
    rows, heads, width = query.shape
    kv_heads = key_cache.shape[2]
    group = heads // kv_heads
    grouped = query.reshape(rows, kv_heads, group, width)
    scores = jnp.einsum(
        "rhgd,rlhd->rhgl", grouped, key_cache, preferred_element_type=jnp.float32
    ) * width ** (-0.5)
    places = jnp.arange(key_cache.shape[1], dtype=jnp.int32)
    valid = places[None, :] < lengths[:, None]
    scores = jnp.where(valid[:, None, None, :], scores, -1e30)
    top = jnp.max(scores, axis=-1, keepdims=True)
    weights = jnp.exp(scores - top)
    probs = (weights / jnp.sum(weights, axis=-1, keepdims=True)).astype(jnp.bfloat16)
    mixed = jnp.einsum("rhgl,rlhd->rhgd", probs, value_cache, preferred_element_type=jnp.float32)
    return mixed.reshape(rows, heads * width).astype(jnp.bfloat16)


def per_device(
    query,
    key_cache,
    value_cache,
    lengths,
    out_weight,
    resid,
    norm_gain,
    gate_weight,
    up_weight,
    down_weight,
):
    attn = attend(query, key_cache, value_cache, lengths)
    block_cols = out_weight.shape[0]
    first_col = lax.axis_index("dev") * block_cols
    cols = lax.dynamic_slice_in_dim(
        lax.all_gather(attn, ("grp", "dev"), axis=0, tiled=True), first_col, block_cols, 1
    )
    proj_terms = jnp.dot(cols, out_weight, preferred_element_type=jnp.float32)
    x = resid.astype(jnp.float32) + lax.psum_scatter(
        proj_terms, "dev", scatter_dimension=0, tiled=True
    )
    width_all = x.shape[1] * lax.axis_size("grp")
    sumsq = lax.psum(jnp.sum(x * x, axis=1), "grp")
    normed = (
        x * lax.rsqrt(sumsq / width_all + 1e-05)[:, None] * norm_gain.astype(jnp.float32)
    ).astype(jnp.bfloat16)
    piece = lax.all_gather(normed, "dev", axis=0, tiled=True)
    half_terms = jnp.concatenate(
        [
            jnp.dot(piece, gate_weight, preferred_element_type=jnp.float32),
            jnp.dot(piece, up_weight, preferred_element_type=jnp.float32),
        ],
        axis=1,
    )
    both = lax.psum(half_terms.astype(jnp.bfloat16), "grp").astype(jnp.float32)
    hidden_cols = gate_weight.shape[1]
    gate = both[:, :hidden_cols]
    up = both[:, hidden_cols:]
    hidden = (jax.nn.silu(gate) * up).astype(jnp.bfloat16)
    ffn_rows = lax.psum_scatter(
        jnp.dot(hidden, down_weight, preferred_element_type=jnp.float32),
        "dev",
        scatter_dimension=0,
        tiled=True,
    )
    return (x + ffn_rows).astype(jnp.bfloat16)


def solution(mesh):
    placed = (
        P(("grp", "dev"), None, None),
        P(("grp", "dev"), None, None, None),
        P(("grp", "dev"), None, None, None),
        P(("grp", "dev")),
        P("dev", "grp"),
        P("dev", "grp"),
        P("grp"),
        P("grp", "dev"),
        P("grp", "dev"),
        P("dev", "grp"),
    )
    return jax.shard_map(
        per_device, mesh=mesh, in_specs=placed, out_specs=P("dev", "grp"), check_vma=False
    )
```

profile of v0, /device:TPU:0, one launch (start us, length us, event | category | flops | bytes accessed | tf_op | source)
XLA Modules:
  0.0 347.9 jit_solution(15746743131024164946)
XLA Ops:
  6.5 0.9 iota_compare_fusion
  7.4 0.7 copy-done
  8.1 1.4 fusion.10
  9.6 0.2 fusion.28
  9.8 2.1 fusion.13
  11.9 0.6 reshape.27
  12.7 56.5 %all-gather.4.cloned.1.call-done = bf16[32,2,8192]{2,1,0:T(2,128)(2,1)} async-done(((bf16[1,2,8192]{2,1,0:T(2,128)(2,1)}), bf16[32,2,8192]{2,1,0:T(2,128)(2,1)}) %all-gather.4.cloned.1.call-update) | async-done | bytes 1048592 | tf_op jit(solution)/shard_map/all_gather | solution.py:41
  69.1 1.5 reshape.28
  70.6 4.1 %fusion.22 = f32[64,4096]{1,0:T(8,128)} fusion(bf16[512,4096]{1,0:T(8,128)(2,1)} %param.14, bf16[64,8192]{1,0:T(8,128)(2,1)S(1)} %reshape.28, s32[]{:T(128)S(6)} %select_n.8), kind=kOutput, calls=%fused_computation.24 | convolution fusion | flops 268435456 | bytes 5308420 | tf_op jit(solution)/shard_map/dot_general | solution.py:43
  74.8 0.6 dynamic-slice
  76.0 91.0 %all-reduce.8.cloned.1.call-done = f32[64,4096]{1,0:T(8,128)} async-done(((f32[64,4096]{1,0:T(8,128)}), f32[64,4096]{1,0:T(8,128)}) %all-reduce.8.cloned.1.call-update) | async-done | bytes 1048592
  167.0 1.1 multiply_reduce_fusion
  168.1 4.9 %psum.14 = f32[4]{0:T(128)S(1)} all-reduce(f32[4]{0:T(128)S(1)} %multiply_reduce_fusion), channel_id=1, replica_groups=mesh['grp'=2,'dev'=16] {'grp'}, use_global_device_ids=true, to_apply=%region_4.5 | all-reduce | flops 4 | bytes 32 | tf_op jit(solution)/shard_map/psum | solution.py:48
  173.0 1.0 fusion.24
  174.0 21.1 %all-gather.1 = bf16[16,4,4096]{2,1,0:T(4,128)(2,1)S(1)} all-gather(bf16[1,4,4096]{2,1,0:T(4,128)(2,1)S(1)} %fusion.24), channel_id=1, replica_groups=mesh['grp'=2,'dev'=16] {'dev'}, dimensions={0}, use_global_device_ids=true | all-gather | bytes 557056 | tf_op jit(solution)/shard_map/all_gather | solution.py:52
  195.1 0.1 reshape.30
  195.2 7.8 %convolution_convert_fusion = bf16[64,1792]{1,0:T(8,128)(2,1)S(1)} fusion(bf16[64,4096]{1,0:T(8,128)(2,1)S(1)} %reshape.30, bf16[4096,1792]{1,0:T(8,128)(2,1)} %param.18), kind=kOutput, calls=%fused_computation.1 | convolution fusion | flops 939638784 | bytes 15433728 | tf_op jit(solution)/shard_map/dot_general | solution.py:56
  203.0 7.8 %convolution_convert_fusion.1 = bf16[64,1792]{1,0:T(8,128)(2,1)S(1)} fusion(bf16[64,4096]{1,0:T(8,128)(2,1)S(1)} %reshape.30, bf16[4096,1792]{1,0:T(8,128)(2,1)} %param.17), kind=kOutput, calls=%fused_computation.2 | convolution fusion | flops 939638784 | bytes 15433728 | tf_op jit(solution)/shard_map/dot_general | solution.py:55
  210.8 0.8 pad_maximum_fusion
  211.7 24.5 %all-reduce.6.cloned.1.call-done = bf16[64,3584]{1,0:T(8,128)(2,1)} async-done(((bf16[64,3584]{1,0:T(8,128)(2,1)}), bf16[64,3584]{1,0:T(8,128)(2,1)}) %all-reduce.6.cloned.1.call-update) | async-done | bytes 458768 | tf_op jit(solution)/shard_map/psum | solution.py:60
  236.3 1.1 convert_element_type.34
  237.3 8.8 %fusion.17 = f32[64,4096]{1,0:T(8,128)} fusion(bf16[1792,4096]{1,0:T(8,128)(2,1)} %param.19, f32[64,3584]{1,0:T(8,128)S(1)} %convert_element_type.34), kind=kOutput, calls=%fused_computation.16 | convolution fusion | flops 940212224 | bytes 16646144 | tf_op jit(solution)/shard_map/dot_general | solution.py:66
  246.2 93.5 %all-reduce.10.cloned.1.call-done = f32[64,4096]{1,0:T(8,128)} async-done(((f32[64,4096]{1,0:T(8,128)}), f32[64,4096]{1,0:T(8,128)}) %all-reduce.10.cloned.1.call-update) | async-done | bytes 1048592
  339.7 1.6 fusion.21
  (17 shorter events, 0.2 us)
Async XLA Ops:
  6.5 1.6 copy-start
  6.5 62.6 %all-gather.4.cloned.1.call-start = ((), (), s32[]{:S(2)}) async-start(), calls=%async_computation.1 | async-start | bytes 1081344 | tf_op jit(solution)/shard_map/all_gather | solution.py:41
  12.6 154.4 %all-reduce.8.cloned.1.call-start = ((), (), s32[]{:S(2)}) async-start(), calls=%async_computation.2 | async-start | bytes 2097152
  12.6 62.1 %copy-start.3 = (u32[32]{0:T(128)S(1)}, u32[32]{0:T(128)}, u32[]{:S(2)}) copy-start(u32[32]{0:T(128)} %constant.33) | copy-start | bytes 388
  12.6 154.4 %copy-start.1 = (bf16[4,4096]{1,0:T(4,128)(2,1)S(1)}, bf16[4,4096]{1,0:T(4,128)(2,1)}, u32[]{:S(2)}) copy-start(bf16[4,4096]{1,0:T(4,128)(2,1)} %param.15) | copy-start | bytes 98308
  12.6 155.4 %copy-start.2 = (bf16[4096]{0:T(1024)(128)(2,1)S(1)}, bf16[4096]{0:T(1024)(128)(2,1)}, u32[]{:S(2)}) copy-start(bf16[4096]{0:T(1024)(128)(2,1)} %param.16) | copy-start | bytes 24580
  74.7 161.6 %all-reduce.6.cloned.1.call-start = ((), (), s32[]{:S(2)}) async-start(), calls=%async_computation | async-start | bytes 917504 | tf_op jit(solution)/shard_map/psum | solution.py:60
  211.7 128.1 %all-reduce.10.cloned.1.call-start = ((), (), s32[]{:S(2)}) async-start(), calls=%async_computation.3 | async-start | bytes 2097152
Sparse Core Ops, SparseCore 0:
  12.7 56.4 all-gather.3
  74.8 92.1 all-reduce.7
  211.8 24.4 all-reduce.5
  246.3 93.3 all-reduce.9
where the time goes:
time: 348 us
  waiting for transfers between devices  266 us (76%)
  matrix products  32.1 us (9%)
  blocking collectives  26 us (7%)
  between operations  13.9 us (4%)
  other arithmetic  6.65 us (2%)
  local copies, waits for them, and re-layouts  3.56 us (1%)
    unnamed x6, waiting for transfers between devices  185 us
    all_gather x1, waiting for transfers between devices, per_device(): lax.all_gather(attn, ('grp', 'dev'), axis=0, tiled=True)  56.5 us
    psum x1, waiting for transfers between devices, per_device(): both = lax.psum(half_terms.astype(jnp.bfloat16), 'grp').astype(jnp.float32)  24.5 us
    all_gather x1, blocking collectives, per_device(): piece = lax.all_gather(normed, 'dev', axis=0, tiled=True)  21.1 us
    dot_general x1, matrix products, per_device(): jnp.dot(hidden, down_weight, preferred_element_type=jnp.float32)  8.84 us
    dot_general x1, matrix products, per_device(): jnp.dot(piece, up_weight, preferred_element_type=jnp.float32)  7.81 us
    dot_general x1, matrix products, per_device(): jnp.dot(piece, gate_weight, preferred_element_type=jnp.float32)  7.81 us
  transfers between devices with their start and end apart: 4, of which 4 were waited for; matrix products, arithmetic and copies ran while one was open for 0% of the time, Pallas kernels for 0%

commit v1 on v0

--- a/solution.py
+++ b/solution.py
@@ -57,7 +57,12 @@
         ],
         axis=1,
     )
-    both = lax.psum(half_terms.astype(jnp.bfloat16), "grp").astype(jnp.float32)
+
+    def perform_results(field_in, axis_tag):
+        mixed_arr = lax.all_gather(field_in, axis_tag)
+        return jnp.sum(mixed_arr, axis=0)
+
+    both = perform_results(half_terms.astype(jnp.bfloat16), "grp").astype(jnp.float32)
     hidden_cols = gate_weight.shape[1]
     gate = both[:, :hidden_cols]
     up = both[:, hidden_cols:]

time: 348 us -> 333 us (0.957)
  waiting for transfers between devices: 266 us -> 238 us
  blocking collectives: 26 us -> 39.5 us
    psum x1 -> x0, waiting for transfers between devices: 24.5 us -> none  [per_device(): both = lax.psum(half_terms.astype(jnp.bfloat16), 'grp').astype(jnp.float32)]
    all_gather x0 -> x1, blocking collectives: none -> 13.4 us  [perform_results(): mixed_arr = lax.all_gather(field_in, axis_tag)]
    unnamed x6 -> x5, waiting for transfers between devices: 185 us -> 182 us
  transfers between devices with their start and end apart: 4 -> 3, of which waited for: 4 -> 3; matrix products, arithmetic and copies ran while one was open for 0% -> 0% of each run, Pallas kernels for 0% -> 0%
where the time goes in v1:
time: 333 us; the launch traced here: 332 us
  waiting for transfers between devices  238 us (71%)
  blocking collectives  39.5 us (12%)
  matrix products  32.1 us (10%)
  between operations  13.9 us (4%)
  other arithmetic  5.19 us (2%)
  local copies, waits for them, and re-layouts  3.56 us (1%)
    unnamed x5, waiting for transfers between devices  182 us
    all_gather x1, waiting for transfers between devices, per_device(): lax.all_gather(attn, ('grp', 'dev'), axis=0, tiled=True)  56.5 us
    all_gather x1, blocking collectives, per_device(): piece = lax.all_gather(normed, 'dev', axis=0, tiled=True)  21.1 us
    all_gather x1, blocking collectives, perform_results(): mixed_arr = lax.all_gather(field_in, axis_tag)  13.4 us
    dot_general x1, matrix products, per_device(): jnp.dot(hidden, down_weight, preferred_element_type=jnp.float32)  8.84 us
    dot_general x1, matrix products, per_device(): jnp.dot(piece, up_weight, preferred_element_type=jnp.float32)  7.81 us
    dot_general x1, matrix products, per_device(): jnp.dot(piece, gate_weight, preferred_element_type=jnp.float32)  7.81 us
  transfers between devices with their start and end apart: 3, of which 3 were waited for; matrix products, arithmetic and copies ran while one was open for 0% of the time, Pallas kernels for 0%

profile of v1, /device:TPU:0, one launch (start us, length us, event | category | flops | bytes accessed | tf_op | source)
XLA Modules:
  0.0 332.4 jit_solution(4016790907575004719)
XLA Ops:
  6.5 0.9 iota_compare_fusion
  7.4 0.7 copy-done
  8.1 1.4 fusion.12
  9.6 0.2 fusion.30
  9.8 2.1 fusion.15
  11.9 0.6 reshape.58
  12.7 56.5 %all-gather.4.cloned.1.call-done = bf16[32,2,8192]{2,1,0:T(2,128)(2,1)} async-done(((bf16[1,2,8192]{2,1,0:T(2,128)(2,1)}), bf16[32,2,8192]{2,1,0:T(2,128)(2,1)}) %all-gather.4.cloned.1.call-update) | async-done | bytes 1048592 | tf_op jit(solution)/shard_map/all_gather | solution.py:41
  69.1 1.5 reshape.59
  70.6 4.1 %fusion.24 = f32[64,4096]{1,0:T(8,128)} fusion(bf16[512,4096]{1,0:T(8,128)(2,1)} %param.14, bf16[64,8192]{1,0:T(8,128)(2,1)S(1)} %reshape.59, s32[]{:T(128)S(6)} %select_n.8), kind=kOutput, calls=%fused_computation.26 | convolution fusion | flops 268435456 | bytes 5308420 | tf_op jit(solution)/shard_map/dot_general | solution.py:43
  74.8 0.6 dynamic-slice
  76.0 91.0 %all-reduce.5.cloned.1.call-done = f32[64,4096]{1,0:T(8,128)} async-done(((f32[64,4096]{1,0:T(8,128)}), f32[64,4096]{1,0:T(8,128)}) %all-reduce.5.cloned.1.call-update) | async-done | bytes 1048592
  167.0 1.1 multiply_reduce_fusion
  168.1 4.9 %psum.7 = f32[4]{0:T(128)S(1)} all-reduce(f32[4]{0:T(128)S(1)} %multiply_reduce_fusion), channel_id=1, replica_groups=mesh['grp'=2,'dev'=16] {'grp'}, use_global_device_ids=true, to_apply=%region_4.5 | all-reduce | flops 4 | bytes 32 | tf_op jit(solution)/shard_map/psum | solution.py:48
  173.0 1.0 fusion.26
  174.0 21.1 %all-gather.1 = bf16[16,4,4096]{2,1,0:T(4,128)(2,1)S(1)} all-gather(bf16[1,4,4096]{2,1,0:T(4,128)(2,1)S(1)} %fusion.26), channel_id=1, replica_groups=mesh['grp'=2,'dev'=16] {'dev'}, dimensions={0}, use_global_device_ids=true | all-gather | bytes 557056 | tf_op jit(solution)/shard_map/all_gather | solution.py:52
  195.1 0.1 reshape.61
  195.2 7.8 %fusion.2 = bf16[1,64,1792]{2,1,0:T(8,128)(2,1)S(1)} fusion(bf16[64,4096]{1,0:T(8,128)(2,1)S(1)} %reshape.61, bf16[4096,1792]{1,0:T(8,128)(2,1)} %param.18), kind=kOutput, calls=%fused_computation.4 | convolution fusion | flops 939638784 | bytes 15433728 | tf_op jit(solution)/shard_map/dot_general | solution.py:56
  203.0 7.8 %fusion.1 = bf16[1,64,1792]{2,1,0:T(8,128)(2,1)S(1)} fusion(bf16[64,4096]{1,0:T(8,128)(2,1)S(1)} %reshape.61, bf16[4096,1792]{1,0:T(8,128)(2,1)} %param.17), kind=kOutput, calls=%fused_computation.3 | convolution fusion | flops 939638784 | bytes 15433728 | tf_op jit(solution)/shard_map/dot_general | solution.py:55
  210.9 13.4 %all_gather.12 = bf16[2,64,3584]{2,1,0:T(8,128)(2,1)S(1)} all-gather(bf16[1,64,3584]{2,1,0:T(8,128)(2,1)S(1)} %pad_maximum_fusion), channel_id=1, replica_groups=mesh['grp'=2,'dev'=16] {'grp'}, dimensions={0}, use_global_device_ids=true | all-gather | bytes 1376256 | tf_op jit(solution)/shard_map/all_gather | solution.py:62
  224.3 0.3 reduce_sum.32
  224.7 0.1 convert_element_type.43
  224.7 8.8 %fusion.19 = f32[64,4096]{1,0:T(8,128)} fusion(bf16[1792,4096]{1,0:T(8,128)(2,1)} %param.19, f32[64,3584]{1,0:T(8,128)S(1)} %convert_element_type.43), kind=kOutput, calls=%fused_computation.18 | convolution fusion | flops 940212224 | bytes 16646144 | tf_op jit(solution)/shard_map/dot_general | solution.py:71
  233.6 90.6 %all-reduce.7.cloned.1.call-done = f32[64,4096]{1,0:T(8,128)} async-done(((f32[64,4096]{1,0:T(8,128)}), f32[64,4096]{1,0:T(8,128)}) %all-reduce.7.cloned.1.call-update) | async-done | bytes 1048592
  324.2 1.6 fusion.23
  (16 shorter events, 0.2 us)
Async XLA Ops:
  6.5 1.6 copy-start
  6.5 62.6 %all-gather.4.cloned.1.call-start = ((), (), s32[]{:S(2)}) async-start(), calls=%async_computation | async-start | bytes 1081344 | tf_op jit(solution)/shard_map/all_gather | solution.py:41
  12.6 154.4 %all-reduce.5.cloned.1.call-start = ((), (), s32[]{:S(2)}) async-start(), calls=%async_computation.1 | async-start | bytes 2097152
  12.6 62.1 %copy-start.3 = (u32[32]{0:T(128)S(1)}, u32[32]{0:T(128)}, u32[]{:S(2)}) copy-start(u32[32]{0:T(128)} %constant.35) | copy-start | bytes 388
  12.6 154.4 %copy-start.1 = (bf16[4,4096]{1,0:T(4,128)(2,1)S(1)}, bf16[4,4096]{1,0:T(4,128)(2,1)}, u32[]{:S(2)}) copy-start(bf16[4,4096]{1,0:T(4,128)(2,1)} %param.15) | copy-start | bytes 98308
  12.6 155.4 %copy-start.2 = (bf16[4096]{0:T(1024)(128)(2,1)S(1)}, bf16[4096]{0:T(1024)(128)(2,1)}, u32[]{:S(2)}) copy-start(bf16[4096]{0:T(1024)(128)(2,1)} %param.16) | copy-start | bytes 24580
  74.7 249.5 %all-reduce.7.cloned.1.call-start = ((), (), s32[]{:S(2)}) async-start(), calls=%async_computation.2 | async-start | bytes 2097152
Sparse Core Ops, SparseCore 0:
  12.7 56.4 all-gather.3
  74.8 92.1 all-reduce.4
  233.7 90.4 all-reduce.6
